TPU v7x, 128 devices: a whole 4x4x4 slice. The times are simulated.
128 devices in a mesh: cells: 64 (over y, z, x), members: 2 (over core).
Axes of the slice: x: 4, y: 4, z: 4, core: 2. Of those that a mesh axis runs over, the one named last changes fastest.
Arguments:
- ensemble: float32 [64, 4, 65536], P('members', None, 'cells')
- speed: float32 [65536], P('cells'), may hold values from 0.1 to 0.85
- direction: int32 [65536], P('cells'), may hold values 0 or 1
- couple: float32 [4, 4], replicated, may hold values from -0.25 to 0.25
- obs_place: int32 [16384], P('cells'), may hold values from 0 to 1023
- obs_field: int32 [16384], P('cells'), may hold values from 0 to 3
- obs_value: float32 [16384], P('cells'), may hold values from -8 to 8
- obs_sigma: float32 [16384], P('cells'), may hold values from 0.5 to 5
- send_count: int32 [64, 64], P('cells'), may hold values from 0 to 32, as said below
Outputs:
- analysis: float32 [64, 4, 65536], P('members', None, 'cells')
- innovation: float32 [16384], P('cells')
Inputs may be any that keep to these rules, and one draw needn't show every extreme that they name: Each row of send_count sums to 256; no entry exceeds 32; in every row four blocks get exactly 32, and one block gets exactly 32 from every row.
All inputs are finite; a program needn't handle non-finite values. No bound on the sum of `direction` on one device may be relied on, other than what follows from the above.
Results may differ from a plain program's by a relative error of at most 0.0001.
Values sent between devices are 32-bit elements; how exact they have to be, the bound alone decides.
A program may use at most 64 MiB of HBM per device.

v0:
```python
import math
import jax
import jax.numpy as jnp
from jax import lax
from jax.sharding import PartitionSpec as P

STEPS = 4
OBS_DEV = 256
CAP = 32
DIFFUSION = 0.05


def padded_2(cells, sides, width):
    for axis, dim in sides:
        count = lax.axis_size(axis)
        ends = count - 1
        head = lax.slice_in_dim(cells, 0, width, axis=dim)
        tail = lax.slice_in_dim(cells, cells.shape[dim] - width, cells.shape[dim], axis=dim)
        cells = jnp.concatenate(
            [
                lax.ppermute(tail, axis, [(i, (i + 1) % count) for i in range(ends)]),
                cells,
                lax.ppermute(head, axis, [((i + 1) % count, i) for i in range(ends)]),
            ],
            axis=dim,
        )
    return cells


def factor_lower(matrix):
    order = matrix.shape[0]
    row_ids = jnp.arange(order, dtype=jnp.int32)

    def column_step(col, lower):
        column = lax.dynamic_slice_in_dim(matrix, col, 1, 1)[:, 0]
        done_row = lax.dynamic_slice_in_dim(lower, col, 1, 0)[0]
        reduced = column - jnp.dot(lower, done_row, precision=lax.Precision.HIGHEST)
        pivot = jnp.sqrt(lax.dynamic_slice_in_dim(reduced, col, 1, 0)[0])
        values = jnp.where(row_ids >= col, reduced / pivot, 0.0)
        return lax.dynamic_update_slice_in_dim(lower, values[:, None], col, 1)

    return lax.fori_loop(0, order, column_step, jnp.zeros_like(matrix))


def invert_lower(lower):
    order = lower.shape[0]
    identity = jnp.eye(order, dtype=jnp.float32)
    diagonal_values = jnp.diagonal(lower)
    nilpotent = identity - lower / diagonal_values[:, None]
    result = identity + nilpotent
    power = nilpotent
    for level in range(max(order - 1, 1).bit_length() - 1):
        power = jnp.dot(power, power, precision=lax.Precision.HIGHEST)
        result = jnp.dot(result, identity + power, precision=lax.Precision.HIGHEST)
    return result / diagonal_values[None, :]


def mixing_matrix(upper_factor, carried, members):
    upper_inverse = invert_lower(upper_factor.T).T
    mean_weights = jnp.dot(upper_inverse, carried, precision=lax.Precision.HIGHEST)
    identity = jnp.eye(members, dtype=jnp.float32)
    spread = math.sqrt(members - 1.0) * upper_inverse
    centering = identity - 1.0 / members
    shifted = jnp.dot(centering, mean_weights, precision=lax.Precision.HIGHEST)
    inner = jnp.dot(
        jnp.dot(centering, spread, precision=lax.Precision.HIGHEST),
        centering,
        precision=lax.Precision.HIGHEST,
    )
    return 1.0 / members + shifted[:, None] + inner


def couple_fields(couple, advanced):
    return advanced + jnp.einsum("fg,kgc->kfc", couple, advanced, precision=lax.Precision.HIGHEST)


def shards(
    ensemble, speed, direction, couple, obs_place, obs_field, obs_value, obs_sigma, send_count
):
    local_members, fields, cells_here = ensemble.shape
    owners = lax.axis_size("cells")
    members = local_members * lax.axis_size("members")
    flag_values = direction.astype(jnp.float32)
    toward_left = speed * flag_values
    toward_right = speed - toward_left
    states = ensemble
    for step_index in range(STEPS):
        padded = padded_2(states, (("cells", 2),), 1)
        left_cells = padded[:, :, :-2]
        right_cells = padded[:, :, 2:]
        advanced = (
            states
            + toward_left * left_cells
            + toward_right * right_cells
            - speed * states
            + DIFFUSION * (left_cells - 2.0 * states + right_cells)
        )
        states = couple_fields(couple, advanced)
    counts_row = send_count[0]
    owner_ends = jnp.cumsum(counts_row)
    starts = owner_ends - counts_row
    slot_ids = jnp.arange(OBS_DEV, dtype=jnp.int32)
    owner_of = jnp.sum((owner_ends[None, :] <= slot_ids[:, None]).astype(jnp.int32), axis=1)
    owner_match = owner_of[:, None] == jnp.arange(owners, dtype=jnp.int32)[None, :]
    start_of = jnp.sum(jnp.where(owner_match, starts[None, :], 0), axis=1)
    position = owner_of * CAP + slot_ids - start_of
    slot_grid = jnp.arange(CAP, dtype=jnp.int32)
    source_slot = jnp.minimum(starts[:, None] + slot_grid[None, :], OBS_DEV - 1)
    live_slot = slot_grid[None, :] < counts_row[:, None]
    request = jnp.where(live_slot, obs_field[source_slot] * cells_here + obs_place[source_slot], 0)
    flat_states = states.reshape(local_members, fields * cells_here)
    asked_slots = lax.all_to_all(request, "cells", split_axis=0, concat_axis=0, tiled=True)
    found_values = jnp.take(flat_states, asked_slots.reshape(-1), axis=1)
    found_values = found_values.reshape(local_members, asked_slots.shape[0], asked_slots.shape[1])
    returned = lax.all_to_all(found_values, "cells", split_axis=1, concat_axis=1, tiled=True)
    local_values = jnp.take(returned.reshape(local_members, owners * CAP), position, axis=1)
    all_values = lax.all_gather(local_values, "members", axis=0, tiled=True)
    center = jnp.mean(all_values, axis=0)
    scaled_anomaly = (all_values - center) / obs_sigma
    innovation = (obs_value - center) / obs_sigma
    augmented = jnp.concatenate([scaled_anomaly, innovation[None, :]], axis=0)
    local_gram = jnp.dot(augmented, augmented.T, precision=lax.Precision.HIGHEST)
    summed_gram = lax.psum(local_gram, "cells")
    diagonal_add = jnp.concatenate(
        [jnp.full((members,), members - 1.0, jnp.float32), jnp.ones((1,), jnp.float32)]
    )
    factor = factor_lower(summed_gram + jnp.diag(diagonal_add)).T
    mixing = mixing_matrix(factor[:members, :members], factor[:members, members], members)
    member_index = lax.axis_index("members")
    own_rows = lax.dynamic_slice_in_dim(mixing, member_index * local_members, local_members, 0)
    analysis = lax.psum_scatter(
        jnp.einsum("kj,kfc->jfc", own_rows, states, precision=lax.Precision.HIGHEST),
        "members",
        scatter_dimension=0,
        tiled=True,
    )
    return (analysis, innovation)


def solution(mesh):
    return jax.shard_map(
        shards,
        mesh=mesh,
        in_specs=(
            P("members", None, "cells"),
            P("cells"),
            P("cells"),
            P(),
            P("cells"),
            P("cells"),
            P("cells"),
            P("cells"),
            P("cells", None),
        ),
        out_specs=(P("members", None, "cells"), P("cells")),
        check_vma=False,
    )
```

profile of v0, /device:TPU:1, one launch (start us, length us, event | category | flops | bytes accessed | tf_op | source)
XLA Modules:
  0.0 626.4 jit_solution(9575588575575584767)
XLA Ops:
  7.2 1.0 fusion.125
  8.2 3.9 collective-permute-start
  12.1 1.3 collective-permute-start.1
  13.4 0.7 copy.33
  14.4 0.7 bitcast_subtract_fusion.1
  15.2 13.2 %gather_fusion = s32[2048]{0:T(1024)S(1)} fusion(s32[256]{0:T(256)S(1)} %copy-done.1, s32[2048]{0:T(1024)S(1)} %broadcast_clamp_fusion.1), kind=kCustom, calls=%fused_computation | custom fusion | bytes 24576 | tf_op jit(solution)/shard_map/gather | solution.py:110
  28.5 13.2 %gather_fusion.1 = s32[2048]{0:T(1024)S(1)} fusion(s32[256]{0:T(256)S(1)} %copy-done.2, s32[2048]{0:T(1024)S(1)} %broadcast_clamp_fusion.1), kind=kCustom, calls=%fused_computation.1 | custom fusion | bytes 24576 | tf_op jit(solution)/shard_map/gather | solution.py:110
  41.8 0.7 fusion.87
  42.5 12.0 %all-to-all-start = ((s32[64,1,32]{2,1,0:T(1,128)}), s32[64,1,32]{2,1,0:T(1,128)S(1)}, u32[]{:S(2)}, u32[]{:S(2)}) async-start(s32[64,1,32]{2,1,0:T(1,128)} %bitcast.3), calls=%async_computation | async-start | bytes 65536 | tf_op jit(solution)/shard_map/all_to_all | solution.py:112
  54.7 2.2 fusion.10
  57.0 2.9 collective-permute-start.2
  59.9 1.3 collective-permute-start.3
  61.3 3.8 collective-permute-done.3
  65.1 2.2 fusion.9
  67.4 2.9 collective-permute-start.4
  70.3 1.3 collective-permute-start.5
  71.6 3.7 collective-permute-done.5
  75.3 2.2 fusion.8
  77.6 4.6 collective-permute-start.6
  82.3 1.5 collective-permute-start.7
  83.8 3.5 collective-permute-done.7
  87.3 2.2 fusion.7
  89.5 0.6 copy.40
  90.7 0.7 reduce.5
  91.5 7.6 %gather_fusion.2 = f32[2048,32]{1,0:T(8,128)} fusion(f32[32,4096]{0,1:T(8,128)S(1)} %bitcast.118, s32[2048]{0:T(1024)S(1)} %broadcast_clamp_fusion), kind=kCustom, calls=%fused_computation.2 | custom fusion | bytes 532480 | tf_op jit(solution)/shard_map/jit(_take)/gather | solution.py:113
  99.1 1.6 fusion.126
  100.7 1.2 reshape.299
  101.9 18.0 %all-to-all-start.1 = ((f32[64,1,1024]{2,1,0:T(1,128)}), f32[64,1,1024]{2,1,0:T(1,128)S(1)}, u32[]{:S(2)}, u32[]{:S(2)}) async-start(f32[64,1,1024]{2,1,0:T(1,128)} %reshape.299), calls=%async_computation.1 | async-start | bytes 524288 | tf_op jit(solution)/shard_map/all_to_all | solution.py:115
  120.0 9.4 %all-to-all-done.1 = f32[64,1,1024]{2,1,0:T(1,128)S(1)} async-done(((f32[64,1,1024]{2,1,0:T(1,128)}), f32[64,1,1024]{2,1,0:T(1,128)S(1)}, u32[]{:S(2)}, u32[]{:S(2)}) %all-to-all-start.1) | async-done | bytes 262176 | tf_op jit(solution)/shard_map/all_to_all | solution.py:115
  129.9 1.3 reduce.6
  131.5 0.7 gather_fusion.3
  132.4 8.5 %all_gather.3 = f32[64,256]{1,0:T(8,128)S(1)} all-gather(f32[32,256]{1,0:T(8,128)S(1)} %copy.36), channel_id=1, replica_groups=mesh['cells'=64,'members'=2] {'members'}, dimensions={0}, use_global_device_ids=true | all-gather | bytes 98304 | tf_op jit(solution)/shard_map/all_gather | solution.py:117
  141.2 288.0 %psum.7 = f32[65,65]{1,0:T(8,128)S(1)} all-reduce(f32[65,65]{1,0:T(8,128)S(1)} %fusion.76), channel_id=1, replica_groups=mesh['cells'=64,'members'=2] {'cells'}, use_global_device_ids=true, to_apply=%region_4.5 | all-reduce | flops 4225 | bytes 33800 | tf_op jit(solution)/shard_map/psum | solution.py:123
  429.4 120.6 %while.14 = (s32[]{:T(128)}, f32[65,65]{1,0:T(8,128)S(1)}, f32[65,65]{0,1:T(8,128)S(1)}, s32[]{:T(128)}, s32[]{:T(128)}) while((s32[]{:T(128)}, f32[65,65]{1,0:T(8,128)S(1)}, f32[65,65]{0,1:T(8,128)S(1)}, s32[]{:T(128)}, s32[]{:T(128)}) %tuple.49), condition=%wide.region_6.7_spmd.clone, body=%wide.region_5.6_spmd.clone.sunk | while | flops 50962 | bytes 40825 | solution.py:42
  429.6 0.6 dynamic_slice.43
  431.3 0.6 dynamic_slice.43
  435.0 0.6 dynamic_slice.43
  438.8 0.6 dynamic_slice.43
  440.6 0.6 dynamic_slice.43
  442.5 0.6 dynamic_slice.43
  444.3 0.6 dynamic_slice.43
  448.0 0.6 dynamic_slice.43
  451.8 0.6 dynamic_slice.43
  453.6 0.6 dynamic_slice.43
  550.1 0.8 gather_fusion.4
  553.6 3.5 fusion.89
  557.1 60.3 %reduce-scatter.2.cloned.1.call-done = f32[32,4,1024]{2,0,1:T(8,128)} async-done(((f32[64,4,1024]{2,0,1:T(8,128)}), f32[32,4,1024]{2,0,1:T(8,128)}) %reduce-scatter.2.cloned.1.call-update) | async-done | bytes 524304 | tf_op jit(solution)/shard_map/reduce_scatter | solution.py:131
  617.4 2.2 copy.39
  (396 shorter events, 73.2 us)
Async XLA Ops:
  7.2 47.5 %copy-start = (f32[4,4]{1,0:T(4,128)S(1)}, f32[4,4]{1,0:T(4,128)}, u32[]{:S(2)}) copy-start(f32[4,4]{1,0:T(4,128)} %param.14) | copy-start | bytes 196
  7.2 8.0 %copy-start.1 = (s32[256]{0:T(256)S(1)}, s32[256]{0:T(256)}, u32[]{:S(2)}) copy-start(s32[256]{0:T(256)} %param.16) | copy-start | bytes 3076
  8.2 46.5 %collective-permute-start = (f32[32,4,1]{2,1,0:T(4,128)S(1)}, f32[32,4,1]{2,1,0:T(4,128)S(1)}, u32[]{:S(2)}, u32[]{:S(2)}) collective-permute-start(f32[32,4,1]{2,1,0:T(4,128)S(1)} %get-tuple-element.122), channel_id=1, source_target_pairs={{0,2},{2,4},{4,6},{6,8},{8,10},{10,12},{12,14},{14,16},{16,18},{18... | collective-permute-start | bytes 1544 | tf_op jit(solution)/shard_map/ppermute | solution.py:21
  12.1 42.5 %collective-permute-start.1 = (f32[32,4,1]{2,1,0:T(4,128)S(1)}, f32[32,4,1]{2,1,0:T(4,128)S(1)}, u32[]{:S(2)}, u32[]{:S(2)}) collective-permute-start(f32[32,4,1]{2,1,0:T(4,128)S(1)} %get-tuple-element.123), channel_id=1, source_target_pairs={{2,0},{4,2},{6,4},{8,6},{10,8},{12,10},{14,12},{16,14},{18,16},{20... | collective-permute-start | bytes 1544 | tf_op jit(solution)/shard_map/ppermute | solution.py:23
  15.2 13.2 %copy-start.2 = (s32[256]{0:T(256)S(1)}, s32[256]{0:T(256)}, u32[]{:S(2)}) copy-start(s32[256]{0:T(256)} %param.15) | copy-start | bytes 3076
  28.4 13.3 %copy-start.8 = (s32[1,64]{1,0:T(1,128)S(1)}, s32[1,64]{1,0:T(1,128)}, u32[]{:S(2)}) copy-start(s32[1,64]{1,0:T(1,128)} %param.19) | copy-start | bytes 772
  28.4 26.1 %copy-start.6 = (s32[1024]{0:T(1024)S(1)}, s32[1024]{0:T(1024)}, u32[]{:S(2)}) copy-start(s32[1024]{0:T(1024)} %param.13) | copy-start | bytes 12292
  28.5 26.1 %copy-start.7 = (f32[1024]{0:T(1024)S(1)}, f32[1024]{0:T(1024)}, u32[]{:S(2)}) copy-start(f32[1024]{0:T(1024)} %param.12) | copy-start | bytes 12292
  28.5 26.2 %copy-start.3 = (f32[32,4,1024]{2,1,0:T(4,128)S(1)}, f32[32,4,1024]{2,1,0:T(4,128)}, u32[]{:S(2)}) copy-start(f32[32,4,1024]{2,1,0:T(4,128)} %param.11) | copy-start | bytes 1572868
  42.5 47.7 %all-to-all-start = ((s32[64,1,32]{2,1,0:T(1,128)}), s32[64,1,32]{2,1,0:T(1,128)S(1)}, u32[]{:S(2)}, u32[]{:S(2)}) async-start(s32[64,1,32]{2,1,0:T(1,128)} %bitcast.3), calls=%async_computation | async-start | bytes 65536 | tf_op jit(solution)/shard_map/all_to_all | solution.py:112
  57.0 4.3 collective-permute-start.2
  59.9 5.2 collective-permute-start.3
  67.4 4.2 collective-permute-start.4
  70.3 5.0 collective-permute-start.5
  77.6 6.1 collective-permute-start.6
  82.3 5.0 collective-permute-start.7
  100.7 40.2 %copy-start.4 = (f32[256]{0:T(256)S(1)}, f32[256]{0:T(256)}, u32[]{:S(2)}) copy-start(f32[256]{0:T(256)} %param.18) | copy-start | bytes 3076
  100.7 40.2 %copy-start.9 = (f32[256]{0:T(256)S(1)}, f32[256]{0:T(256)}, u32[]{:S(2)}) copy-start(f32[256]{0:T(256)} %param.17) | copy-start | bytes 3076
  101.9 327.3 %copy-start.10 = (f32[65]{0:T(128)S(1)}, f32[65]{0:T(128)}, u32[]{:S(2)}) copy-start(f32[65]{0:T(128)} %constant.99.clone.1) | copy-start | bytes 784
  101.9 27.5 %all-to-all-start.1 = ((f32[64,1,1024]{2,1,0:T(1,128)}), f32[64,1,1024]{2,1,0:T(1,128)S(1)}, u32[]{:S(2)}, u32[]{:S(2)}) async-start(f32[64,1,1024]{2,1,0:T(1,128)} %reshape.299), calls=%async_computation.1 | async-start | bytes 524288 | tf_op jit(solution)/shard_map/all_to_all | solution.py:115
  119.9 497.5 %reduce-scatter.2.cloned.1.call-start = ((), (), s32[]{:S(2)}) async-start(), calls=%async_computation.3 | async-start | bytes 1572864 | tf_op jit(solution)/shard_map/reduce_scatter | solution.py:131
  140.9 416.1 %copy-start.5 = (f32[256]{0:T(256)}, f32[256]{0:T(256)S(1)}, u32[]{:S(2)}) copy-start(f32[256]{0:T(256)S(1)} %get-tuple-element.127) | copy-start | bytes 3076
Sparse Core Ops, SparseCore 0:
  557.2 60.1 reduce-scatter.1
where the time goes:
time: 632 us; the launch traced here: 626 us
  blocking collectives  297 us (47%)
  local copies, waits for them, and re-layouts  107 us (17%)
  waiting for transfers between devices  80.7 us (13%)
  starting transfers between devices  49.8 us (8%)
  loops' own time  47.1 us (7%)
  matrix products  24.6 us (4%)
  between operations  14.6 us (2%)
    psum x1, blocking collectives, shards(): summed_gram = lax.psum(local_gram, 'cells')  288 us
    reduce_scatter x1, waiting for transfers between devices, shards(): lax.psum_scatter(jnp.einsum('kj,kfc->jfc', own_rows, states, precision=la...  60.3 us
    another operation x1, loops' own time, factor_lower(): return lax.fori_loop(0, order, column_step, jnp.zeros_like(matrix))  47.1 us
    dynamic_slice x65, local copies, waits for them, and re-layouts, column_step(): pivot = jnp.sqrt(lax.dynamic_slice_in_dim(reduced, col, 1, 0)[0])  40.3 us
    all_to_all x1, starting transfers between devices, shards(): lax.all_to_all(found_values, 'cells', split_axis=1, concat_axis=1, tiled=...  18 us
    dynamic_update_slice x65, local copies, waits for them, and re-layouts, column_step(): return lax.dynamic_update_slice_in_dim(lower, values[:, None], col, 1)  16.2 us
    ppermute x4, starting transfers between devices, padded_2(): lax.ppermute(tail, axis, [(i, (i + 1) % count) for i in range(ends)])  14.4 us
    gather x1, local copies, waits for them, and re-layouts, shards(): obs_field[source_slot] * cells_here + obs_place[source_slot]  13.2 us
  transfers between devices with their start and end apart: 11, of which 5 were waited for; matrix products, arithmetic and copies ran while one was open for 6% of the time, Pallas kernels for 0%

commit v1 on v0

--- a/solution.py
+++ b/solution.py
@@ -120,7 +120,7 @@
     innovation = (obs_value - center) / obs_sigma
     augmented = jnp.concatenate([scaled_anomaly, innovation[None, :]], axis=0)
     local_gram = jnp.dot(augmented, augmented.T, precision=lax.Precision.HIGHEST)
-    summed_gram = lax.psum(local_gram, "cells")
+    summed_gram = jnp.sum(lax.all_gather(local_gram, "cells"), axis=0)
     diagonal_add = jnp.concatenate(
         [jnp.full((members,), members - 1.0, jnp.float32), jnp.ones((1,), jnp.float32)]
     )

time: 632 us -> 356 us (0.56)
  blocking collectives: 297 us -> 8.45 us
  waiting for transfers between devices: 80.7 us -> 90.9 us
    psum x1 -> x0, blocking collectives: 288 us -> none  [shards(): summed_gram = lax.psum(local_gram, 'cells')]
    all_gather x0 -> x1, waiting for transfers between devices: none -> 60.2 us  [shards(): summed_gram = jnp.sum(lax.all_gather(local_gram, 'cells'), axis=0)]
    reduce_scatter x1, waiting for transfers between devices: 60.3 us -> 10.3 us  [shards(): lax.psum_scatter(jnp.einsum('kj,kfc->jfc', own_rows, states, precision=la...]
  transfers between devices with their start and end apart: 11 -> 12, of which waited for: 5 -> 6; matrix products, arithmetic and copies ran while one was open for 6% -> 11% of each run, Pallas kernels for 0% -> 0%
where the time goes in v1:
time: 356 us; the launch traced here: 351 us
  local copies, waits for them, and re-layouts  107 us (30%)
  waiting for transfers between devices  90.9 us (26%)
  starting transfers between devices  49.7 us (14%)
  loops' own time  47.1 us (13%)
  matrix products  25.1 us (7%)
  between operations  14.6 us (4%)
  blocking collectives  8.45 us (2%)
  other arithmetic  7.93 us (2%)
    all_gather x1, waiting for transfers between devices, shards(): summed_gram = jnp.sum(lax.all_gather(local_gram, 'cells'), axis=0)  60.2 us
    another operation x1, loops' own time, factor_lower(): return lax.fori_loop(0, order, column_step, jnp.zeros_like(matrix))  47.1 us
    dynamic_slice x65, local copies, waits for them, and re-layouts, column_step(): pivot = jnp.sqrt(lax.dynamic_slice_in_dim(reduced, col, 1, 0)[0])  40.3 us
    all_to_all x1, starting transfers between devices, shards(): lax.all_to_all(found_values, 'cells', split_axis=1, concat_axis=1, tiled=...  17.9 us
    dynamic_update_slice x65, local copies, waits for them, and re-layouts, column_step(): return lax.dynamic_update_slice_in_dim(lower, values[:, None], col, 1)  16.2 us
    ppermute x4, starting transfers between devices, padded_2(): lax.ppermute(tail, axis, [(i, (i + 1) % count) for i in range(ends)])  14.4 us
    gather x1, local copies, waits for them, and re-layouts, shards(): obs_field[source_slot] * cells_here + obs_place[source_slot]  13.2 us
    gather x1, local copies, waits for them, and re-layouts, shards(): obs_place[source_slot]  13.2 us
  transfers between devices with their start and end apart: 12, of which 6 were waited for; matrix products, arithmetic and copies ran while one was open for 11% of the time, Pallas kernels for 0%

profile of v1, /device:TPU:1, one launch (start us, length us, event | category | flops | bytes accessed | tf_op | source)
XLA Modules:
  0.0 350.9 jit_solution(2498511892987684119)
XLA Ops:
  7.2 1.0 fusion.124
  8.2 3.9 %collective-permute-start = (f32[32,4,1]{2,1,0:T(4,128)S(1)}, f32[32,4,1]{2,1,0:T(4,128)S(1)}, u32[]{:S(2)}, u32[]{:S(2)}) collective-permute-start(f32[32,4,1]{2,1,0:T(4,128)S(1)} %get-tuple-element.116), channel_id=1, source_target_pairs={{0,2},{2,4},{4,6},{6,8},{8,10},{10,12},{12,14},{14,16},{16,18},{18... | collective-permute-start | bytes 1544 | tf_op jit(solution)/shard_map/ppermute | solution.py:21
  12.1 1.3 collective-permute-start.1
  13.4 0.7 copy.33
  14.4 0.7 bitcast_subtract_fusion.1
  15.2 13.2 %gather_fusion = s32[2048]{0:T(1024)S(1)} fusion(s32[256]{0:T(256)S(1)} %copy-done.1, s32[2048]{0:T(1024)S(1)} %broadcast_clamp_fusion.1), kind=kCustom, calls=%fused_computation | custom fusion | bytes 24576 | tf_op jit(solution)/shard_map/gather | solution.py:110
  28.5 13.2 %gather_fusion.1 = s32[2048]{0:T(1024)S(1)} fusion(s32[256]{0:T(256)S(1)} %copy-done.2, s32[2048]{0:T(1024)S(1)} %broadcast_clamp_fusion.1), kind=kCustom, calls=%fused_computation.1 | custom fusion | bytes 24576 | tf_op jit(solution)/shard_map/gather | solution.py:110
  41.8 0.7 fusion.86
  42.5 12.0 %all-to-all-start = ((s32[64,1,32]{2,1,0:T(1,128)}), s32[64,1,32]{2,1,0:T(1,128)S(1)}, u32[]{:S(2)}, u32[]{:S(2)}) async-start(s32[64,1,32]{2,1,0:T(1,128)} %bitcast.3), calls=%async_computation | async-start | bytes 65536 | tf_op jit(solution)/shard_map/all_to_all | solution.py:112
  54.7 2.2 fusion.10
  56.9 2.9 collective-permute-start.2
  59.9 1.3 collective-permute-start.3
  61.2 3.9 %collective-permute-done.3 = f32[32,4,1]{2,1,0:T(4,128)S(1)} collective-permute-done((f32[32,4,1]{2,1,0:T(4,128)S(1)}, f32[32,4,1]{2,1,0:T(4,128)S(1)}, u32[]{:S(2)}, u32[]{:S(2)}) %collective-permute-start.3) | collective-permute-done | bytes 544 | tf_op jit(solution)/shard_map/ppermute | solution.py:23
  65.1 2.2 fusion.9
  67.4 2.9 collective-permute-start.4
  70.3 1.3 collective-permute-start.5
  71.7 3.6 %collective-permute-done.5 = f32[32,4,1]{2,1,0:T(4,128)S(1)} collective-permute-done((f32[32,4,1]{2,1,0:T(4,128)S(1)}, f32[32,4,1]{2,1,0:T(4,128)S(1)}, u32[]{:S(2)}, u32[]{:S(2)}) %collective-permute-start.5) | collective-permute-done | bytes 544 | tf_op jit(solution)/shard_map/ppermute | solution.py:23
  75.3 2.2 fusion.8
  77.6 4.6 %collective-permute-start.6 = (f32[32,4,1]{2,1,0:T(4,128)S(1)}, f32[32,4,1]{2,1,0:T(4,128)S(1)}, u32[]{:S(2)}, u32[]{:S(2)}) collective-permute-start(f32[32,4,1]{2,1,0:T(4,128)S(1)} %get-tuple-element.110), channel_id=1, source_target_pairs={{0,2},{2,4},{4,6},{6,8},{8,10},{10,12},{12,14},{14,16},{16,18},{18... | collective-permute-start | bytes 1544 | tf_op jit(solution)/shard_map/ppermute | solution.py:21
  82.2 1.5 collective-permute-start.7
  83.7 3.5 collective-permute-done.7
  87.2 2.2 fusion.7
  89.4 0.6 copy.40
  90.6 0.7 reduce.6
  91.5 7.6 %gather_fusion.2 = f32[2048,32]{1,0:T(8,128)} fusion(f32[32,4096]{0,1:T(8,128)S(1)} %bitcast.120, s32[2048]{0:T(1024)S(1)} %broadcast_clamp_fusion), kind=kCustom, calls=%fused_computation.2 | custom fusion | bytes 532480 | tf_op jit(solution)/shard_map/jit(_take)/gather | solution.py:113
  99.1 1.6 fusion.125
  100.7 1.2 reshape.303
  101.8 17.9 %all-to-all-start.1 = ((f32[64,1,1024]{2,1,0:T(1,128)}), f32[64,1,1024]{2,1,0:T(1,128)S(1)}, u32[]{:S(2)}, u32[]{:S(2)}) async-start(f32[64,1,1024]{2,1,0:T(1,128)} %reshape.303), calls=%async_computation.1 | async-start | bytes 524288 | tf_op jit(solution)/shard_map/all_to_all | solution.py:115
  119.8 9.4 %all-to-all-done.1 = f32[64,1,1024]{2,1,0:T(1,128)S(1)} async-done(((f32[64,1,1024]{2,1,0:T(1,128)}), f32[64,1,1024]{2,1,0:T(1,128)S(1)}, u32[]{:S(2)}, u32[]{:S(2)}) %all-to-all-start.1) | async-done | bytes 262176 | tf_op jit(solution)/shard_map/all_to_all | solution.py:115
  129.7 1.3 reduce.7
  131.3 0.7 gather_fusion.3
  132.2 8.5 %all_gather.9 = f32[64,256]{1,0:T(8,128)S(1)} all-gather(f32[32,256]{1,0:T(8,128)S(1)} %copy.36), channel_id=1, replica_groups=mesh['cells'=64,'members'=2] {'members'}, dimensions={0}, use_global_device_ids=true | all-gather | bytes 98304 | tf_op jit(solution)/shard_map/all_gather | solution.py:117
  140.8 0.8 convolution_bitcast_fusion.5
  141.7 60.2 %all-gather.4.cloned.1.call-done = f32[64,65,65]{2,1,0:T(8,128)} async-done(((f32[1,65,65]{2,1,0:T(8,128)}), f32[64,65,65]{2,1,0:T(8,128)}) %all-gather.4.cloned.1.call-update) | async-done | bytes 1081616 | tf_op jit(solution)/shard_map/all_gather | solution.py:123
  201.9 1.9 reduce_sum.42
  203.9 120.6 %while.14 = (s32[]{:T(128)}, f32[65,65]{1,0:T(8,128)S(1)}, f32[65,65]{0,1:T(8,128)S(1)}, s32[]{:T(128)}, s32[]{:T(128)}) while((s32[]{:T(128)}, f32[65,65]{1,0:T(8,128)S(1)}, f32[65,65]{0,1:T(8,128)S(1)}, s32[]{:T(128)}, s32[]{:T(128)}) %tuple.47), condition=%wide.region_6.7_spmd.clone, body=%wide.region_5.6_spmd.clone.sunk | while | flops 50962 | bytes 40825 | solution.py:42
  204.1 0.6 dynamic_slice.43
  207.7 0.6 dynamic_slice.43
  211.4 0.6 dynamic_slice.43
  213.3 0.6 dynamic_slice.43
  217.0 0.6 dynamic_slice.43
  220.7 0.6 dynamic_slice.43
  222.6 0.6 dynamic_slice.43
  224.4 0.6 dynamic_slice.43
  324.6 0.8 gather_fusion.4
  328.1 3.5 fusion.88
  331.6 10.3 %reduce-scatter.2.cloned.1.call-done = f32[32,4,1024]{2,0,1:T(8,128)} async-done(((f32[64,4,1024]{2,0,1:T(8,128)}), f32[32,4,1024]{2,0,1:T(8,128)}) %reduce-scatter.2.cloned.1.call-update) | async-done | bytes 524304 | tf_op jit(solution)/shard_map/reduce_scatter | solution.py:131
  341.9 2.2 copy.39
  (399 shorter events, 74.3 us)
Async XLA Ops:
  7.2 47.5 %copy-start = (f32[4,4]{1,0:T(4,128)S(1)}, f32[4,4]{1,0:T(4,128)}, u32[]{:S(2)}) copy-start(f32[4,4]{1,0:T(4,128)} %param.14) | copy-start | bytes 196
  7.2 8.0 %copy-start.1 = (s32[256]{0:T(256)S(1)}, s32[256]{0:T(256)}, u32[]{:S(2)}) copy-start(s32[256]{0:T(256)} %param.16) | copy-start | bytes 3076
  8.2 46.4 %collective-permute-start = (f32[32,4,1]{2,1,0:T(4,128)S(1)}, f32[32,4,1]{2,1,0:T(4,128)S(1)}, u32[]{:S(2)}, u32[]{:S(2)}) collective-permute-start(f32[32,4,1]{2,1,0:T(4,128)S(1)} %get-tuple-element.116), channel_id=1, source_target_pairs={{0,2},{2,4},{4,6},{6,8},{8,10},{10,12},{12,14},{14,16},{16,18},{18... | collective-permute-start | bytes 1544 | tf_op jit(solution)/shard_map/ppermute | solution.py:21
  12.1 42.5 %collective-permute-start.1 = (f32[32,4,1]{2,1,0:T(4,128)S(1)}, f32[32,4,1]{2,1,0:T(4,128)S(1)}, u32[]{:S(2)}, u32[]{:S(2)}) collective-permute-start(f32[32,4,1]{2,1,0:T(4,128)S(1)} %get-tuple-element.117), channel_id=1, source_target_pairs={{2,0},{4,2},{6,4},{8,6},{10,8},{12,10},{14,12},{16,14},{18,16},{20... | collective-permute-start | bytes 1544 | tf_op jit(solution)/shard_map/ppermute | solution.py:23
  15.2 13.2 %copy-start.2 = (s32[256]{0:T(256)S(1)}, s32[256]{0:T(256)}, u32[]{:S(2)}) copy-start(s32[256]{0:T(256)} %param.15) | copy-start | bytes 3076
  28.4 13.3 %copy-start.8 = (s32[1,64]{1,0:T(1,128)S(1)}, s32[1,64]{1,0:T(1,128)}, u32[]{:S(2)}) copy-start(s32[1,64]{1,0:T(1,128)} %param.19) | copy-start | bytes 772
  28.4 26.1 %copy-start.6 = (s32[1024]{0:T(1024)S(1)}, s32[1024]{0:T(1024)}, u32[]{:S(2)}) copy-start(s32[1024]{0:T(1024)} %param.13) | copy-start | bytes 12292
  28.5 26.1 %copy-start.7 = (f32[1024]{0:T(1024)S(1)}, f32[1024]{0:T(1024)}, u32[]{:S(2)}) copy-start(f32[1024]{0:T(1024)} %param.12) | copy-start | bytes 12292
  28.5 26.2 %copy-start.3 = (f32[32,4,1024]{2,1,0:T(4,128)S(1)}, f32[32,4,1024]{2,1,0:T(4,128)}, u32[]{:S(2)}) copy-start(f32[32,4,1024]{2,1,0:T(4,128)} %param.11) | copy-start | bytes 1572868
  42.5 47.6 %all-to-all-start = ((s32[64,1,32]{2,1,0:T(1,128)}), s32[64,1,32]{2,1,0:T(1,128)S(1)}, u32[]{:S(2)}, u32[]{:S(2)}) async-start(s32[64,1,32]{2,1,0:T(1,128)} %bitcast.3), calls=%async_computation | async-start | bytes 65536 | tf_op jit(solution)/shard_map/all_to_all | solution.py:112
  56.9 4.2 %collective-permute-start.2 = (f32[32,4,1]{2,1,0:T(4,128)S(1)}, f32[32,4,1]{2,1,0:T(4,128)S(1)}, u32[]{:S(2)}, u32[]{:S(2)}) collective-permute-start(f32[32,4,1]{2,1,0:T(4,128)S(1)} %get-tuple-element.114), channel_id=1, source_target_pairs={{0,2},{2,4},{4,6},{6,8},{8,10},{10,12},{12,14},{14,16},{16,18},{18... | collective-permute-start | bytes 1544 | tf_op jit(solution)/shard_map/ppermute | solution.py:21
  59.9 5.2 %collective-permute-start.3 = (f32[32,4,1]{2,1,0:T(4,128)S(1)}, f32[32,4,1]{2,1,0:T(4,128)S(1)}, u32[]{:S(2)}, u32[]{:S(2)}) collective-permute-start(f32[32,4,1]{2,1,0:T(4,128)S(1)} %get-tuple-element.115), channel_id=1, source_target_pairs={{2,0},{4,2},{6,4},{8,6},{10,8},{12,10},{14,12},{16,14},{18,16},{20... | collective-permute-start | bytes 1544 | tf_op jit(solution)/shard_map/ppermute | solution.py:23
  67.4 4.3 %collective-permute-start.4 = (f32[32,4,1]{2,1,0:T(4,128)S(1)}, f32[32,4,1]{2,1,0:T(4,128)S(1)}, u32[]{:S(2)}, u32[]{:S(2)}) collective-permute-start(f32[32,4,1]{2,1,0:T(4,128)S(1)} %get-tuple-element.112), channel_id=1, source_target_pairs={{0,2},{2,4},{4,6},{6,8},{8,10},{10,12},{12,14},{14,16},{16,18},{18... | collective-permute-start | bytes 1544 | tf_op jit(solution)/shard_map/ppermute | solution.py:21
  70.3 5.0 %collective-permute-start.5 = (f32[32,4,1]{2,1,0:T(4,128)S(1)}, f32[32,4,1]{2,1,0:T(4,128)S(1)}, u32[]{:S(2)}, u32[]{:S(2)}) collective-permute-start(f32[32,4,1]{2,1,0:T(4,128)S(1)} %get-tuple-element.113), channel_id=1, source_target_pairs={{2,0},{4,2},{6,4},{8,6},{10,8},{12,10},{14,12},{16,14},{18,16},{20... | collective-permute-start | bytes 1544 | tf_op jit(solution)/shard_map/ppermute | solution.py:23
  77.6 6.1 %collective-permute-start.6 = (f32[32,4,1]{2,1,0:T(4,128)S(1)}, f32[32,4,1]{2,1,0:T(4,128)S(1)}, u32[]{:S(2)}, u32[]{:S(2)}) collective-permute-start(f32[32,4,1]{2,1,0:T(4,128)S(1)} %get-tuple-element.110), channel_id=1, source_target_pairs={{0,2},{2,4},{4,6},{6,8},{8,10},{10,12},{12,14},{14,16},{16,18},{18... | collective-permute-start | bytes 1544 | tf_op jit(solution)/shard_map/ppermute | solution.py:21
  82.2 5.0 %collective-permute-start.7 = (f32[32,4,1]{2,1,0:T(4,128)S(1)}, f32[32,4,1]{2,1,0:T(4,128)S(1)}, u32[]{:S(2)}, u32[]{:S(2)}) collective-permute-start(f32[32,4,1]{2,1,0:T(4,128)S(1)} %get-tuple-element.111), channel_id=1, source_target_pairs={{2,0},{4,2},{6,4},{8,6},{10,8},{12,10},{14,12},{16,14},{18,16},{20... | collective-permute-start | bytes 1544 | tf_op jit(solution)/shard_map/ppermute | solution.py:23
  100.6 40.1 %copy-start.4 = (f32[256]{0:T(256)S(1)}, f32[256]{0:T(256)}, u32[]{:S(2)}) copy-start(f32[256]{0:T(256)} %param.18) | copy-start | bytes 3076
  100.7 40.0 %copy-start.9 = (f32[256]{0:T(256)S(1)}, f32[256]{0:T(256)}, u32[]{:S(2)}) copy-start(f32[256]{0:T(256)} %param.17) | copy-start | bytes 3076
  101.8 27.4 %all-to-all-start.1 = ((f32[64,1,1024]{2,1,0:T(1,128)}), f32[64,1,1024]{2,1,0:T(1,128)S(1)}, u32[]{:S(2)}, u32[]{:S(2)}) async-start(f32[64,1,1024]{2,1,0:T(1,128)} %reshape.303), calls=%async_computation.1 | async-start | bytes 524288 | tf_op jit(solution)/shard_map/all_to_all | solution.py:115
  119.7 82.1 %all-gather.4.cloned.1.call-start = ((), (), s32[]{:S(2)}) async-start(), calls=%async_computation.4 | async-start | bytes 2396160 | tf_op jit(solution)/shard_map/all_gather | solution.py:123
  131.3 72.4 %copy-start.10 = (f32[65]{0:T(128)S(1)}, f32[65]{0:T(128)}, u32[]{:S(2)}) copy-start(f32[65]{0:T(128)} %constant.99.clone.1) | copy-start | bytes 784
  140.7 184.7 %copy-start.5 = (f32[256]{0:T(256)}, f32[256]{0:T(256)S(1)}, u32[]{:S(2)}) copy-start(f32[256]{0:T(256)S(1)} %get-tuple-element.121) | copy-start | bytes 3076
  141.6 200.2 %reduce-scatter.2.cloned.1.call-start = ((), (), s32[]{:S(2)}) async-start(), calls=%async_computation.3 | async-start | bytes 1572864 | tf_op jit(solution)/shard_map/reduce_scatter | solution.py:131
Sparse Core Ops, SparseCore 0:
  141.7 60.0 all-gather.3
  331.7 10.1 reduce-scatter.1
